TPU v7x, 32 devices: a whole 2x2x4 slice. The times are simulated.
32 devices in a mesh: scene: 2 (over x), seq: 16 (over z, y, core).
Axes of the slice: x: 2, y: 2, z: 4, core: 2. Of those that a mesh axis runs over, the one named last changes fastest.
Arguments:
- tokens: bfloat16 [2, 4096, 1024], P('scene', 'seq'), may hold values from -6 to 6
- surface_mask: int32 [2, 4096], P('scene', 'seq'), may hold values 0 or 1
- out_grad: bfloat16 [2, 4096, 1024], P('scene', 'seq'), may hold values from -6 to 6
- w_query: bfloat16 [1024, 1024], replicated, may hold values from -0.1875 to 0.1875
- w_key: bfloat16 [1024, 1024], replicated, may hold values from -0.1875 to 0.1875
- w_value: bfloat16 [1024, 1024], replicated, may hold values from -0.1875 to 0.1875
- w_out: bfloat16 [1024, 1024], replicated, may hold values from -6 to 6
- w_up: bfloat16 [1024, 4096], replicated, may hold values from -0.1875 to 0.1875
- w_down: bfloat16 [4096, 1024], replicated, may hold values from -0.09375 to 0.09375
- b_query: float32 [1024], replicated, may hold values from -3 to 3
- b_value: float32 [1024], replicated, may hold values from -3 to 3
- b_out: float32 [1024], replicated, may hold values from -3 to 3
- b_up: float32 [4096], replicated, may hold values from -3 to 3
- b_down: float32 [1024], replicated, may hold values from -3 to 3
- gain_one: float32 [1024], replicated, may hold values from 0.1 to 1.9
- shift_one: float32 [1024], replicated, may hold values from -3 to 3
- gain_two: float32 [1024], replicated, may hold values from 0.1 to 1.9
- shift_two: float32 [1024], replicated, may hold values from -3 to 3
Outputs:
- block_out: bfloat16 [2, 4096, 1024], P('scene', 'seq')
- tokens_grad: bfloat16 [2, 4096, 1024], P('scene', 'seq')
- query_grad: float32 [1024, 1024], P(('scene', 'seq'))
- key_grad: float32 [1024, 1024], P(('scene', 'seq'))
- value_grad: float32 [1024, 1024], P(('scene', 'seq'))
- out_proj_grad: float32 [1024, 1024], P(('scene', 'seq'))
- up_grad: float32 [1024, 4096], P(('scene', 'seq'))
- down_grad: float32 [4096, 1024], P(('scene', 'seq'))
- query_bias_grad: float32 [1024], P(('scene', 'seq'))
- value_bias_grad: float32 [1024], P(('scene', 'seq'))
- out_bias_grad: float32 [1024], P(('scene', 'seq'))
- up_bias_grad: float32 [4096], P(('scene', 'seq'))
- down_bias_grad: float32 [1024], P(('scene', 'seq'))
- gain_one_grad: float32 [1024], P(('scene', 'seq'))
- shift_one_grad: float32 [1024], P(('scene', 'seq'))
- gain_two_grad: float32 [1024], P(('scene', 'seq'))
- shift_two_grad: float32 [1024], P(('scene', 'seq'))
All inputs are finite; a program needn't handle non-finite values. No bound on the sum of `surface_mask` on one device may be relied on, other than what follows from the above.
Results may differ from a plain program's by a relative error of at most 0.014.
Values may be sent and summed in bfloat16 or wider, within the bound.
A program may use at most 320 MiB of HBM per device.

v0:
```python
import jax
import jax.numpy as jnp
from jax import lax
from jax.sharding import PartitionSpec as P

HEADS = 16
HEAD_DIM = 64
norm_eps = 1e-05
score_scale = 0.125
gelu_coef = 0.7978845608028654


def norm_rows(values, gain, shift):
    row_mean = jnp.mean(values, axis=-1, keepdims=True)
    centred = values - row_mean
    row_var = jnp.mean(centred * centred, axis=-1, keepdims=True)
    return centred * lax.rsqrt(row_var + norm_eps) * gain + shift


def gelu_tanh(values):
    return (
        0.5 * values * (1.0 + jnp.tanh(gelu_coef * (values + 0.044715 * values * values * values)))
    )


def matmul(left, right):
    return jnp.dot(left, right, preferred_element_type=jnp.float32)


def matmul_tn(left, right):
    return lax.dot_general(
        left, right, (((0,), (0,)), ((), ())), preferred_element_type=jnp.float32
    )


def matmul_nt(left, right):
    return lax.dot_general(
        left, right, (((1,), (1,)), ((), ())), preferred_element_type=jnp.float32
    )


def take_pair(array_in, pair_index):
    pair_width = 2 * HEAD_DIM
    sliced = lax.dynamic_slice_in_dim(array_in, pair_index * pair_width, pair_width, 2)
    return sliced.reshape(sliced.shape[:2] + (2, HEAD_DIM))


def take_stats(array_in, pair_index):
    return lax.dynamic_slice_in_dim(array_in, pair_index * 2, 2, 1)


def join_pairs(stacked):
    moved = jnp.moveaxis(stacked, 0, 2)
    return moved.reshape(moved.shape[:2] + (moved.shape[2] * moved.shape[3],))


def join_stats(stacked):
    moved = jnp.moveaxis(stacked, 0, 1)
    return moved.reshape((moved.shape[0], moved.shape[1] * moved.shape[2], moved.shape[3]))


def merge_heads(pair_part):
    return pair_part.reshape(pair_part.shape[:2] + (2 * HEAD_DIM,))


def attend(q_scene, k_gathered, v_gathered):

    def attend_pair_step(unused, pair_index):
        q_pair = take_pair(q_scene, pair_index)
        k_pair = take_pair(k_gathered, pair_index)
        v_pair = take_pair(v_gathered, pair_index)
        scores = (
            jnp.einsum("sqhe,skhe->shqk", q_pair, k_pair, preferred_element_type=jnp.float32)
            * score_scale
        )
        row_max = jnp.max(scores, axis=-1, keepdims=True)
        shifted = jnp.exp(scores - row_max)
        row_sum = jnp.sum(shifted, axis=-1, keepdims=True)
        prob_low = (shifted / row_sum).astype(jnp.bfloat16)
        pair_out = jnp.einsum(
            "shqk,skhe->sqhe", prob_low, v_pair, preferred_element_type=jnp.float32
        )
        pair_lse = (row_max + jnp.log(row_sum))[..., 0]
        return (unused, (merge_heads(pair_out), pair_lse))

    pair_count = HEADS // 2
    _, (pair_outs, pair_lses) = lax.scan(
        attend_pair_step, jnp.zeros((), jnp.float32), jnp.arange(pair_count, dtype=jnp.int32)
    )
    return (join_pairs(pair_outs), join_stats(pair_lses))


def query_side(q_scene, k_gathered, v_gathered, row_lse, att_grad):

    def query_pair_step(unused, pair_index):
        q_pair = take_pair(q_scene, pair_index)
        k_pair = take_pair(k_gathered, pair_index)
        v_pair = take_pair(v_gathered, pair_index)
        d_pair = take_pair(att_grad, pair_index)
        l_pair = take_stats(row_lse, pair_index)
        scores = (
            jnp.einsum("sqhe,skhe->shqk", q_pair, k_pair, preferred_element_type=jnp.float32)
            * score_scale
        )
        attn_prob = jnp.exp(scores - l_pair[..., None])
        dprob = jnp.einsum("sqhe,skhe->shqk", d_pair, v_pair, preferred_element_type=jnp.float32)
        row_delta = jnp.sum(attn_prob * dprob, axis=-1)
        dscore = (attn_prob * (dprob - row_delta[..., None])).astype(jnp.bfloat16)
        q_part = (
            jnp.einsum("shqk,skhe->sqhe", dscore, k_pair, preferred_element_type=jnp.float32)
            * score_scale
        )
        results = (merge_heads(q_part), row_delta)
        prob_low = attn_prob.astype(jnp.bfloat16)
        k_part = (
            jnp.einsum("shqk,sqhe->skhe", dscore, q_pair, preferred_element_type=jnp.float32)
            * score_scale
        )
        v_part = jnp.einsum("shqk,sqhe->skhe", prob_low, d_pair, preferred_element_type=jnp.float32)
        results = results + (merge_heads(k_part), merge_heads(v_part))
        return (unused, results)

    pair_count = HEADS // 2
    _, results = lax.scan(
        query_pair_step, jnp.zeros((), jnp.float32), jnp.arange(pair_count, dtype=jnp.int32)
    )
    return results


def on_device(
    tokens,
    surface_mask,
    out_grad,
    w_query,
    w_key,
    w_value,
    w_out,
    w_up,
    w_down,
    b_query,
    b_value,
    b_out,
    b_up,
    b_down,
    gain_one,
    shift_one,
    gain_two,
    shift_two,
):
    scenes, local_len, model_width = tokens.shape
    row_count = scenes * local_len
    flat_rows = tokens.astype(jnp.float32).reshape(row_count, model_width)
    normed, norm_one_pull = jax.vjp(norm_rows, flat_rows, gain_one, shift_one)
    normed_low = normed.astype(jnp.bfloat16)
    q_low = (matmul(normed_low, w_query) + b_query).astype(jnp.bfloat16)
    k_low = matmul(normed_low, w_key).astype(jnp.bfloat16)
    v_low = (matmul(normed_low, w_value) + b_value).astype(jnp.bfloat16)
    q_scene = q_low.reshape(scenes, local_len, model_width)
    k_scene = k_low.reshape(scenes, local_len, model_width)
    v_scene = v_low.reshape(scenes, local_len, model_width)
    k_gathered, v_gathered = (
        lax.all_gather(k_scene, "seq", axis=1, tiled=True),
        lax.all_gather(v_scene, "seq", axis=1, tiled=True),
    )
    attended, row_lse = attend(q_scene, k_gathered, v_gathered)
    att_low = attended.reshape(row_count, model_width).astype(jnp.bfloat16)
    residual = flat_rows + matmul(att_low, w_out) + b_out
    normed_two, norm_two_pull = jax.vjp(norm_rows, residual, gain_two, shift_two)
    normed_two_low = normed_two.astype(jnp.bfloat16)
    hidden = matmul(normed_two_low, w_up) + b_up
    activated, gelu_pull = jax.vjp(gelu_tanh, hidden)
    act_low = activated.astype(jnp.bfloat16)
    block_rows = residual + matmul(act_low, w_down) + b_down
    block_out = block_rows.reshape(scenes, local_len, model_width).astype(jnp.bfloat16)
    masked_f = out_grad.astype(jnp.float32) * surface_mask.astype(jnp.float32)[..., None]
    masked_rows = masked_f.reshape(row_count, model_width)
    masked_low = masked_rows.astype(jnp.bfloat16)
    grad_down = matmul_tn(act_low, masked_low)
    grad_bdown = jnp.sum(masked_rows, axis=0)
    act_grad = matmul_nt(masked_low, w_down)
    hidden_low = gelu_pull(act_grad)[0].astype(jnp.bfloat16)
    grad_up = matmul_tn(normed_two_low, hidden_low)
    grad_bup = jnp.sum(hidden_low.astype(jnp.float32), axis=0)
    norm_two_in = matmul_nt(hidden_low, w_up)
    resid_part, grad_gain_two, grad_shift_two = norm_two_pull(norm_two_in)
    resid_grad = masked_rows + resid_part
    resid_low = resid_grad.astype(jnp.bfloat16)
    grad_out = matmul_tn(att_low, resid_low)
    grad_bout = jnp.sum(resid_low.astype(jnp.float32), axis=0)
    att_grad = (
        matmul_nt(resid_low, w_out).astype(jnp.bfloat16).reshape(scenes, local_len, model_width)
    )
    q_parts, delta_parts, k_parts, v_parts = query_side(
        q_scene, k_gathered, v_gathered, row_lse, att_grad
    )
    k_summed, v_summed = (
        lax.psum_scatter(
            k_parts.astype(jnp.bfloat16), "seq", scatter_dimension=2, tiled=True
        ).astype(jnp.float32),
        lax.psum_scatter(
            v_parts.astype(jnp.bfloat16), "seq", scatter_dimension=2, tiled=True
        ).astype(jnp.float32),
    )
    k_grad = join_pairs(k_summed)
    v_grad = join_pairs(v_summed)
    q_grad = join_pairs(q_parts)
    q_grad_low = q_grad.reshape(row_count, model_width).astype(jnp.bfloat16)
    k_grad_low = k_grad.reshape(row_count, model_width).astype(jnp.bfloat16)
    v_grad_low = v_grad.reshape(row_count, model_width).astype(jnp.bfloat16)
    grad_query = matmul_tn(normed_low, q_grad_low)
    grad_key = matmul_tn(normed_low, k_grad_low)
    grad_value = matmul_tn(normed_low, v_grad_low)
    grad_bquery = jnp.sum(q_grad_low.astype(jnp.float32), axis=0)
    grad_bvalue = jnp.sum(v_grad_low.astype(jnp.float32), axis=0)
    norm_one_in = (
        matmul_nt(q_grad_low, w_query)
        + matmul_nt(k_grad_low, w_key)
        + matmul_nt(v_grad_low, w_value)
    )
    token_part, grad_gain_one, grad_shift_one = norm_one_pull(norm_one_in)
    tokens_grad = (
        (resid_grad + token_part).reshape(scenes, local_len, model_width).astype(jnp.bfloat16)
    )
    (
        sum_query,
        sum_key,
        sum_value,
        sum_out,
        sum_bquery,
        sum_bvalue,
        sum_bout,
        sum_gain_one,
        sum_shift_one,
        sum_up,
        sum_down,
        sum_bup,
        sum_bdown,
        sum_gain_two,
        sum_shift_two,
    ) = (
        lax.psum_scatter(grad_query, ("scene", "seq"), scatter_dimension=0, tiled=True),
        lax.psum_scatter(grad_key, ("scene", "seq"), scatter_dimension=0, tiled=True),
        lax.psum_scatter(grad_value, ("scene", "seq"), scatter_dimension=0, tiled=True),
        lax.psum_scatter(grad_out, ("scene", "seq"), scatter_dimension=0, tiled=True),
        lax.psum_scatter(grad_bquery, ("scene", "seq"), scatter_dimension=0, tiled=True),
        lax.psum_scatter(grad_bvalue, ("scene", "seq"), scatter_dimension=0, tiled=True),
        lax.psum_scatter(grad_bout, ("scene", "seq"), scatter_dimension=0, tiled=True),
        lax.psum_scatter(grad_gain_one, ("scene", "seq"), scatter_dimension=0, tiled=True),
        lax.psum_scatter(grad_shift_one, ("scene", "seq"), scatter_dimension=0, tiled=True),
        lax.psum_scatter(grad_up, ("scene", "seq"), scatter_dimension=0, tiled=True),
        lax.psum_scatter(grad_down, ("scene", "seq"), scatter_dimension=0, tiled=True),
        lax.psum_scatter(grad_bup, ("scene", "seq"), scatter_dimension=0, tiled=True),
        lax.psum_scatter(grad_bdown, ("scene", "seq"), scatter_dimension=0, tiled=True),
        lax.psum_scatter(grad_gain_two, ("scene", "seq"), scatter_dimension=0, tiled=True),
        lax.psum_scatter(grad_shift_two, ("scene", "seq"), scatter_dimension=0, tiled=True),
    )
    return (
        block_out,
        tokens_grad,
        sum_query,
        sum_key,
        sum_value,
        sum_out,
        sum_up,
        sum_down,
        sum_bquery,
        sum_bvalue,
        sum_bout,
        sum_bup,
        sum_bdown,
        sum_gain_one,
        sum_shift_one,
        sum_gain_two,
        sum_shift_two,
    )


def solution(mesh):
    placed = (
        P("scene", "seq", None),
        P("scene", "seq"),
        P("scene", "seq", None),
        P(),
        P(),
        P(),
        P(),
        P(),
        P(),
        P(),
        P(),
        P(),
        P(),
        P(),
        P(),
        P(),
        P(),
        P(),
    )
    return jax.shard_map(
        on_device,
        mesh=mesh,
        in_specs=placed,
        out_specs=(
            P("scene", "seq", None),
            P("scene", "seq", None),
            P(("scene", "seq"), None),
            P(("scene", "seq"), None),
            P(("scene", "seq"), None),
            P(("scene", "seq"), None),
            P(("scene", "seq"), None),
            P(("scene", "seq"), None),
            P(("scene", "seq")),
            P(("scene", "seq")),
            P(("scene", "seq")),
            P(("scene", "seq")),
            P(("scene", "seq")),
            P(("scene", "seq")),
            P(("scene", "seq")),
            P(("scene", "seq")),
            P(("scene", "seq")),
        ),
        check_vma=False,
    )
```

profile of v0, /device:TPU:9, one launch (start us, length us, event | category | flops | bytes accessed | tf_op | source)
XLA Modules:
  0.0 1661.1 jit_solution(7076041561755759142)
XLA Ops:
  10.0 3.4 convolution_convert_fusion.1
  15.2 2.3 fusion.21
  18.6 70.9 %all-gather.7.cloned.1.call-done = bf16[4096,1024]{1,0:T(8,128)(2,1)} async-done(((bf16[256,1024]{1,0:T(8,128)(2,1)}), bf16[4096,1024]{1,0:T(8,128)(2,1)}) %all-gather.7.cloned.1.call-update) | async-done | bytes 8388624 | tf_op jit(solution)/shard_map/all_gather | solution.py:162
  89.5 11.3 copy.44
  100.7 64.6 %all-gather.5.cloned.1.call-done = bf16[4096,1024]{1,0:T(8,128)(2,1)} async-done(((bf16[256,1024]{1,0:T(8,128)(2,1)}), bf16[4096,1024]{1,0:T(8,128)(2,1)}) %all-gather.5.cloned.1.call-update) | async-done | bytes 8388624 | tf_op jit(solution)/shard_map/all_gather | solution.py:163
  165.4 11.3 copy.42
  176.8 71.2 %while.26 = (s32[]{:T(128)}, bf16[8,1,256,128]{2,3,1,0:T(8,128)(2,1)S(1)}, f32[8,1,2,256]{3,2,1,0:T(2,128)S(1)}, s32[8]{0:T(128)S(1)}, bf16[1,4096,1024]{1,2,0:T...) while((s32[]{:T(128)}, ...), condition=%wide.region_5.6_spmd, body=%wide.region_2.5_spmd.sunk | while | flops 555744768 | bytes 31867072 | solution.py:87
  178.9 1.7 constant_dynamic-slice_fusion.13
  183.5 2.2 fusion.118
  187.8 1.7 constant_dynamic-slice_fusion.13
  192.4 2.2 fusion.118
  201.3 2.2 fusion.118
  210.2 2.2 fusion.118
  219.1 2.2 fusion.118
  228.0 2.2 fusion.118
  236.9 2.2 fusion.118
  245.8 2.2 fusion.118
  248.1 2.6 fusion.57
  251.0 6.0 convolution_add_fusion
  257.1 6.5 convert_reduce_fusion
  263.6 3.2 multiply_reduce_fusion.2
  271.5 234.4 %while.27 = (s32[]{:T(128)}, bf16[8,1,256,128]{2,3,1,0:T(8,128)(2,1)}, bf16[8,1,4096,128]{2,3,1,0:T(8,128)(2,1)}, bf16[8,1,4096,128]{2,3,1,0:T(8,128)(2,1)}, s32...) while((s32[]{:T(128)}, ...), condition=%wide.region_12.13_spmd, body=%wide.region_10.12_spmd.sunk | while | flops 1360068096 | bytes 123546016 | solution.py:124
  278.4 4.9 multiply_reduce_fusion.8
  284.1 7.9 multiply_convert_fusion.5
  292.0 4.3 fusion.130
  307.7 4.9 multiply_reduce_fusion.8
  313.4 7.9 multiply_convert_fusion.5
  321.3 4.3 fusion.130
  337.0 4.9 multiply_reduce_fusion.8
  342.7 7.9 multiply_convert_fusion.5
  350.6 4.3 fusion.130
  366.3 4.9 multiply_reduce_fusion.8
  372.0 7.9 multiply_convert_fusion.5
  379.9 4.3 fusion.130
  395.6 4.9 multiply_reduce_fusion.8
  401.3 7.9 multiply_convert_fusion.5
  409.2 4.3 fusion.130
  424.8 4.9 multiply_reduce_fusion.8
  430.5 7.9 multiply_convert_fusion.5
  438.5 4.3 fusion.130
  454.2 4.9 multiply_reduce_fusion.8
  459.9 7.9 multiply_convert_fusion.5
  467.8 4.3 fusion.130
  483.5 4.9 multiply_reduce_fusion.8
  489.2 7.9 multiply_convert_fusion.5
  497.1 4.3 fusion.130
  507.1 2.7 fusion.60
  511.2 2.9 fusion.49
  514.2 95.1 %reduce-scatter.11.cloned.1.call-done = bf16[8,1,256,128]{2,3,1,0:T(8,128)(2,1)} async-done(((bf16[8,1,4096,128]{2,3,1,0:T(8,128)(2,1)}), bf16[8,1,256,128]{2,3,1,0:T(8,128)(2,1)}) %reduce-scatter.11.cloned.1.call-update) | async-done | bytes 524304 | tf_op jit(solution)/shard_map/reduce_scatter | solution.py:200
  609.4 3.8 fusion.45
  613.3 104.6 %reduce-scatter.9.cloned.1.call-done = bf16[8,1,256,128]{2,3,1,0:T(8,128)(2,1)} async-done(((bf16[8,1,4096,128]{2,3,1,0:T(8,128)(2,1)}), bf16[8,1,256,128]{2,3,1,0:T(8,128)(2,1)}) %reduce-scatter.9.cloned.1.call-update) | async-done | bytes 524304 | tf_op jit(solution)/shard_map/reduce_scatter | solution.py:197
  717.9 3.9 fusion.47
  721.9 10.8 fusion.39
  733.4 10.2 fusion.44
  745.2 2.5 fusion.59
  747.8 8.4 fusion.23
  759.8 40.0 %all-reduce.9 = (f32[1024]{0:T(1024)S(1)}, f32[1024]{0:T(1024)S(1)}, f32[1024]{0:T(1024)S(1)}, f32[4096]{0:T(1024)S(1)}, f32[1024]{0:T(1024)S(1)}, /*index=5*/f3...) all-reduce(f32[1024]{0:T(1024)S(1)} %bitcast.240, ...), channel_id=12, replica_groups=mesh['scene'=2,'seq'=16] {'scene','seq'}, use_global_device_ids=true, to_apply=%region_24.25.clone | all-reduce | flops 12288 | bytes 98304
  805.1 2.9 fusion.37
  808.0 38.4 %reduce-scatter.19.cloned.1.call-done = f32[32,1024]{1,0:T(8,128)} async-done(((f32[1024,1024]{1,0:T(8,128)}), f32[32,1024]{1,0:T(8,128)}) %reduce-scatter.19.cloned.1.call-update) | async-done | bytes 131088 | tf_op jit(solution)/shard_map/reduce_scatter | solution.py:244
  846.4 139.8 %reduce-scatter.13.cloned.1.call-done = f32[32,1024]{1,0:T(8,128)} async-done(((f32[1024,1024]{1,0:T(8,128)}), f32[32,1024]{1,0:T(8,128)}) %reduce-scatter.13.cloned.1.call-update) | async-done | bytes 131088 | tf_op jit(solution)/shard_map/reduce_scatter | solution.py:241
  986.2 140.4 %reduce-scatter.17.cloned.1.call-done = f32[32,1024]{1,0:T(8,128)} async-done(((f32[1024,1024]{1,0:T(8,128)}), f32[32,1024]{1,0:T(8,128)}) %reduce-scatter.17.cloned.1.call-update) | async-done | bytes 131088 | tf_op jit(solution)/shard_map/reduce_scatter | solution.py:243
  1126.6 140.2 %reduce-scatter.15.cloned.1.call-done = f32[32,1024]{1,0:T(8,128)} async-done(((f32[1024,1024]{1,0:T(8,128)}), f32[32,1024]{1,0:T(8,128)}) %reduce-scatter.15.cloned.1.call-update) | async-done | bytes 131088 | tf_op jit(solution)/shard_map/reduce_scatter | solution.py:242
  1266.8 198.9 %reduce-scatter.23.cloned.1.call-done = f32[128,1024]{1,0:T(8,128)} async-done(((f32[4096,1024]{1,0:T(8,128)}), f32[128,1024]{1,0:T(8,128)}) %reduce-scatter.23.cloned.1.call-update) | async-done | bytes 524304 | tf_op jit(solution)/shard_map/reduce_scatter | solution.py:251
  1465.7 188.2 %reduce-scatter.21.cloned.1.call-done = f32[32,4096]{1,0:T(8,128)} async-done(((f32[1024,4096]{1,0:T(8,128)}), f32[32,4096]{1,0:T(8,128)}) %reduce-scatter.21.cloned.1.call-update) | async-done | bytes 524304 | tf_op jit(solution)/shard_map/reduce_scatter | solution.py:250
  (390 shorter events, 155.1 us)
Async XLA Ops:
  7.2 6.3 copy-start
  7.2 6.3 copy-start.4
  7.2 6.3 copy-start.26
  7.2 6.3 copy-start.32
  7.2 6.3 copy-start.47
  7.2 82.2 %all-gather.7.cloned.1.call-start = ((), (), s32[]{:S(2)}) async-start(), calls=%async_computation.17 | async-start | bytes 8912896 | tf_op jit(solution)/shard_map/all_gather | solution.py:162
  8.6 6.6 copy-start.30
  10.0 5.1 copy-start.41
  10.0 5.2 copy-start.34
  10.0 5.2 copy-start.45
  10.0 5.2 copy-start.48
  13.4 151.9 %all-gather.5.cloned.1.call-start = ((), (), s32[]{:S(2)}) async-start(), calls=%async_computation.16 | async-start | bytes 8912896 | tf_op jit(solution)/shard_map/all_gather | solution.py:163
  15.1 594.3 %reduce-scatter.11.cloned.1.call-start = ((), (), s32[]{:S(2)}) async-start(), calls=%async_computation.9 | async-start | bytes 8912896 | tf_op jit(solution)/shard_map/reduce_scatter | solution.py:200
  176.8 71.3 %copy-start.36 = (f32[1024]{0:T(1024)S(1)}, f32[1024]{0:T(1024)}, u32[]{:S(2)}) copy-start(f32[1024]{0:T(1024)} %param.33) | copy-start | bytes 12292
  248.0 9.0 copy-start.13
  248.0 3.0 copy-start.25
  248.0 3.0 copy-start.28
  248.1 9.0 slice-start.2
  250.7 16.1 copy-start.6
  251.0 6.1 copy-start.10
  251.0 6.0 slice-start.3
  251.0 12.6 slice-start
  257.0 6.6 copy-start.15
  257.1 6.5 slice-start.1
  263.6 3.2 copy-start.22
  266.8 3.1 copy-start.20
  271.5 6.9 copy-start.23
  278.4 5.7 copy-start.1
  292.0 4.4 copy-start.3
  300.7 6.9 copy-start.23
  307.7 5.7 copy-start.1
  321.3 4.4 copy-start.3
  330.0 6.9 copy-start.23
  337.0 5.7 copy-start.1
  350.6 4.4 copy-start.3
  359.3 6.9 copy-start.23
  366.3 5.7 copy-start.1
  379.9 4.4 copy-start.3
  388.6 6.9 copy-start.23
  395.6 5.7 copy-start.1
  409.2 4.4 copy-start.3
  417.9 6.9 copy-start.23
  424.8 5.7 copy-start.1
  438.5 4.4 copy-start.3
  447.2 6.9 copy-start.23
  454.2 5.7 copy-start.1
  467.8 4.4 copy-start.3
  476.5 6.9 copy-start.23
  483.5 5.7 copy-start.1
  497.1 4.4 copy-start.3
  505.9 212.0 %reduce-scatter.9.cloned.1.call-start = ((), (), s32[]{:S(2)}) async-start(), calls=%async_computation.8 | async-start | bytes 8912896 | tf_op jit(solution)/shard_map/reduce_scatter | solution.py:197
  506.5 340.0 %reduce-scatter.19.cloned.1.call-start = ((), (), s32[]{:S(2)}) async-start(), calls=%async_computation.13 | async-start | bytes 4325376 | tf_op jit(solution)/shard_map/reduce_scatter | solution.py:244
  509.9 476.4 %reduce-scatter.13.cloned.1.call-start = ((), (), s32[]{:S(2)}) async-start(), calls=%async_computation.10 | async-start | bytes 4325376 | tf_op jit(solution)/shard_map/reduce_scatter | solution.py:241
  514.2 612.4 %reduce-scatter.17.cloned.1.call-start = ((), (), s32[]{:S(2)}) async-start(), calls=%async_computation.12 | async-start | bytes 4325376 | tf_op jit(solution)/shard_map/reduce_scatter | solution.py:243
  613.2 653.6 %reduce-scatter.15.cloned.1.call-start = ((), (), s32[]{:S(2)}) async-start(), calls=%async_computation.11 | async-start | bytes 4325376 | tf_op jit(solution)/shard_map/reduce_scatter | solution.py:242
  717.9 4.0 copy-start.11
  721.8 743.9 %reduce-scatter.23.cloned.1.call-start = ((), (), s32[]{:S(2)}) async-start(), calls=%async_computation.15 | async-start | bytes 17301504 | tf_op jit(solution)/shard_map/reduce_scatter | solution.py:251
  732.8 921.1 %reduce-scatter.21.cloned.1.call-start = ((), (), s32[]{:S(2)}) async-start(), calls=%async_computation.14 | async-start | bytes 17301504 | tf_op jit(solution)/shard_map/reduce_scatter | solution.py:250
  743.6 4.1 copy-start.49
  743.6 4.1 copy-start.7
  747.8 8.4 copy-start.16
  747.8 8.7 copy-start.19
  747.8 8.7 copy-start.21
  757.3 47.9 %copy-start.40 = (f32[256]{0:T(256)S(1)}, f32[256]{0:T(256)}, u32[]{:S(2)}) copy-start(f32[256]{0:T(256)} %copy-done.39) | copy-start | bytes 3076
  (35 other events, 58.0 us)
Sparse Core Ops, SparseCore 0:
  13.5 75.8 all-gather.6
  92.2 73.1 all-gather.4
  506.0 103.3 reduce-scatter.10
  613.3 104.5 reduce-scatter.8
  720.6 125.7 reduce-scatter.18
  849.1 137.0 reduce-scatter.12
  989.1 137.4 reduce-scatter.16
  1129.4 137.2 reduce-scatter.14
  1269.7 195.9 reduce-scatter.22
  1468.4 185.3 reduce-scatter.20
where the time goes:
time: 1670 us; the launch traced here: 1660 us
  waiting for transfers between devices  1180 us (71%)
  matrix products  203 us (12%)
  local copies, waits for them, and re-layouts  118 us (7%)
  other arithmetic  85 us (5%)
  blocking collectives  40 us (2%)
  loops' own time  17 us (1%)
    reduce_scatter x1, waiting for transfers between devices, on_device(): lax.psum_scatter(grad_down, ('scene', 'seq'), scatter_dimension=0, tiled=...  199 us
    reduce_scatter x1, waiting for transfers between devices, on_device(): lax.psum_scatter(grad_up, ('scene', 'seq'), scatter_dimension=0, tiled=True)  188 us
    reduce_scatter x1, waiting for transfers between devices, on_device(): lax.psum_scatter(grad_value, ('scene', 'seq'), scatter_dimension=0, tiled...  140 us
    reduce_scatter x1, waiting for transfers between devices, on_device(): lax.psum_scatter(grad_key, ('scene', 'seq'), scatter_dimension=0, tiled=T...  140 us
    reduce_scatter x1, waiting for transfers between devices, on_device(): lax.psum_scatter(grad_query, ('scene', 'seq'), scatter_dimension=0, tiled...  140 us
    reduce_scatter x1, waiting for transfers between devices, on_device(): lax.psum_scatter(k_parts.astype(jnp.bfloat16), 'seq', scatter_dimension=2...  105 us
    reduce_scatter x1, waiting for transfers between devices, on_device(): lax.psum_scatter(v_parts.astype(jnp.bfloat16), 'seq', scatter_dimension=2...  95.1 us
    all_gather x1, waiting for transfers between devices, on_device(): lax.all_gather(k_scene, 'seq', axis=1, tiled=True)  70.9 us
  transfers between devices with their start and end apart: 10, of which 10 were waited for; matrix products, arithmetic and copies ran while one was open for 4% of the time, Pallas kernels for 0%

commit v1 on v0

--- a/solution.py
+++ b/solution.py
@@ -8,6 +8,19 @@
 norm_eps = 1e-05
 score_scale = 0.125
 gelu_coef = 0.7978845608028654
+
+
+def ring_gather(x, axis, dim):
+    ways = lax.axis_size(axis)
+    up = [(d, (d + 1) % ways) for d in range(ways)]
+    down = [(d, (d - 1) % ways) for d in range(ways)]
+    earlier, later = ([x], [x])
+    for _ in range(ways // 2):
+        earlier.append(lax.ppermute(earlier[-1], axis, up))
+    for _ in range((ways - 1) // 2):
+        later.append(lax.ppermute(later[-1], axis, down))
+    line = jnp.concatenate([*earlier[::-1], *later[1:]], axis=dim)
+    return jnp.roll(line, (lax.axis_index(axis) - ways // 2) * x.shape[dim], axis=dim)
 
 
 def norm_rows(values, gain, shift):
@@ -159,7 +172,7 @@
     k_scene = k_low.reshape(scenes, local_len, model_width)
     v_scene = v_low.reshape(scenes, local_len, model_width)
     k_gathered, v_gathered = (
-        lax.all_gather(k_scene, "seq", axis=1, tiled=True),
+        ring_gather(k_scene, "seq", 1),
         lax.all_gather(v_scene, "seq", axis=1, tiled=True),
     )
     attended, row_lse = attend(q_scene, k_gathered, v_gathered)

time: 1670 us -> 1770 us (1.060)
  matrix products: 203 us -> 258 us
  local copies, waits for them, and re-layouts: 118 us -> 170 us
  waiting for transfers between devices: 1180 us -> 1150 us
  starting transfers between devices: 0.62 us -> 22.5 us
    ppermute x0 -> x15, waiting for transfers between devices: none -> 102 us  [the longest x7 77.4 us: ring_gather(): later.append(lax.ppermute(later[-1], axis, down))]
    reduce_scatter x1, waiting for transfers between devices: 38.4 us -> 140 us  [on_device(): lax.psum_scatter(grad_out, ('scene', 'seq'), scatter_dimension=0, tiled=T...]
    reduce_scatter x1, waiting for transfers between devices: 140 us -> 38.4 us  [on_device(): lax.psum_scatter(grad_query, ('scene', 'seq'), scatter_dimension=0, tiled...]
    all_gather x1 -> x0, waiting for transfers between devices: 70.9 us -> none  [on_device(): lax.all_gather(k_scene, 'seq', axis=1, tiled=True)]
    all_gather x1, waiting for transfers between devices: 64.6 us -> 0.01 us  [on_device(): lax.all_gather(v_scene, 'seq', axis=1, tiled=True)]
    unnamed x107 -> x166, local copies, waits for them, and re-layouts: 10.5 us -> 52.8 us
    dot_general x8, matrix products: 10.2 us -> 36.2 us  [query_pair_step(): jnp.einsum('sqhe,skhe->shqk', d_pair, v_pair, preferred_element_type=jnp....]
    ppermute x0 -> x15, starting transfers between devices: none -> 21.9 us  [the longest x8 15.7 us: ring_gather(): earlier.append(lax.ppermute(earlier[-1], axis, up))]
  transfers between devices with their start and end apart: 10 -> 24, of which waited for: 10 -> 19; matrix products, arithmetic and copies ran while one was open for 4% -> 7% of each run, Pallas kernels for 0% -> 0%
where the time goes in v1:
time: 1770 us; the launch traced here: 1760 us
  waiting for transfers between devices  1150 us (65%)
  matrix products  258 us (15%)
  local copies, waits for them, and re-layouts  170 us (10%)
  other arithmetic  86.4 us (5%)
  blocking collectives  39.7 us (2%)
  starting transfers between devices  22.5 us (1%)
    reduce_scatter x1, waiting for transfers between devices, on_device(): lax.psum_scatter(grad_up, ('scene', 'seq'), scatter_dimension=0, tiled=True)  200 us
    reduce_scatter x1, waiting for transfers between devices, on_device(): lax.psum_scatter(grad_down, ('scene', 'seq'), scatter_dimension=0, tiled=...  188 us
    reduce_scatter x1, waiting for transfers between devices, on_device(): lax.psum_scatter(grad_key, ('scene', 'seq'), scatter_dimension=0, tiled=T...  140 us
    reduce_scatter x1, waiting for transfers between devices, on_device(): lax.psum_scatter(grad_value, ('scene', 'seq'), scatter_dimension=0, tiled...  140 us
    reduce_scatter x1, waiting for transfers between devices, on_device(): lax.psum_scatter(grad_out, ('scene', 'seq'), scatter_dimension=0, tiled=T...  140 us
    reduce_scatter x1, waiting for transfers between devices, on_device(): lax.psum_scatter(v_parts.astype(jnp.bfloat16), 'seq', scatter_dimension=2...  105 us
    reduce_scatter x1, waiting for transfers between devices, on_device(): lax.psum_scatter(k_parts.astype(jnp.bfloat16), 'seq', scatter_dimension=2...  96.4 us
    ppermute x7, waiting for transfers between devices, ring_gather(): later.append(lax.ppermute(later[-1], axis, down))  77.4 us
  transfers between devices with their start and end apart: 24, of which 19 were waited for; matrix products, arithmetic and copies ran while one was open for 7% of the time, Pallas kernels for 0%

profile of v1, /device:TPU:9, one launch (start us, length us, event | category | flops | bytes accessed | tf_op | source)
XLA Modules:
  0.0 1759.1 jit_solution(11596859226097761331)
XLA Ops:
  17.2 6.1 collective-permute-done
  25.9 9.9 collective-permute-done.1
  40.2 6.2 collective-permute-start.9
  50.6 24.0 %collective-permute-done.9 = bf16[1,256,1024]{2,1,0:T(8,128)(2,1)S(1)} collective-permute-done((bf16[1,256,1024]{2,1,0:T(8,128)(2,1)S(1)}, bf16[1,256,1024]{2,1,0:T(8,128)(2,1)S(1)}, u32[]{:S(2)}, u32[]{:S(2)}) %collective-permute-start.9) | collective-permute-done | bytes 524320 | tf_op jit(solution)/shard_map/ppermute | solution.py:21
  76.4 28.7 %collective-permute-done.10 = bf16[1,256,1024]{2,1,0:T(8,128)(2,1)S(1)} collective-permute-done((bf16[1,256,1024]{2,1,0:T(8,128)(2,1)S(1)}, bf16[1,256,1024]{2,1,0:T(8,128)(2,1)S(1)}, u32[]{:S(2)}, u32[]{:S(2)}) %collective-permute-start.10) | collective-permute-done | bytes 524320 | tf_op jit(solution)/shard_map/ppermute | solution.py:21
  106.9 7.9 collective-permute-done.11
  120.3 13.0 collective-permute-done.12
  135.2 3.1 fusion.21
  142.3 5.0 collective-permute-done.7
  189.1 7.6 constant_dynamic-slice_fusion.7
  196.6 11.8 copy.44
  208.4 11.7 copy.42
  220.2 71.3 %while.26 = (s32[]{:T(128)}, bf16[8,1,256,128]{2,3,1,0:T(8,128)(2,1)S(1)}, f32[8,1,2,256]{3,2,1,0:T(2,128)S(1)}, s32[8]{0:T(128)S(1)}, bf16[1,4096,1024]{1,2,0:T...) while((s32[]{:T(128)}, ...), condition=%wide.region_5.6_spmd, body=%wide.region_2.5_spmd.sunk | while | flops 555744768 | bytes 31867072 | solution.py:100
  294.6 6.0 convolution_add_fusion
  300.6 6.5 convert_reduce_fusion
  307.2 4.1 multiply_reduce_fusion.2
  319.8 282.4 %while.27 = (s32[]{:T(128)}, bf16[8,1,256,128]{2,3,1,0:T(8,128)(2,1)}, bf16[8,1,4096,128]{2,3,1,0:T(8,128)(2,1)}, bf16[8,1,4096,128]{2,3,1,0:T(8,128)(2,1)}, s32...) while((s32[]{:T(128)}, ...), condition=%wide.region_12.13_spmd, body=%wide.region_10.12_spmd.sunk | while | flops 1360068096 | bytes 81602872 | solution.py:137
  324.7 4.5 fusion.130
  330.8 6.6 multiply_reduce_fusion.8
  337.4 7.9 multiply_convert_fusion.5
  348.6 4.2 fusion.131
  360.0 4.5 fusion.130
  366.0 6.6 multiply_reduce_fusion.8
  372.7 7.9 multiply_convert_fusion.5
  383.9 4.2 fusion.131
  395.3 4.5 fusion.130
  401.4 6.6 multiply_reduce_fusion.8
  408.0 7.9 multiply_convert_fusion.5
  419.2 4.2 fusion.131
  430.6 4.5 fusion.130
  436.7 6.6 multiply_reduce_fusion.8
  443.3 7.9 multiply_convert_fusion.5
  454.5 4.2 fusion.131
  465.9 4.5 fusion.130
  471.9 6.6 multiply_reduce_fusion.8
  478.5 7.9 multiply_convert_fusion.5
  489.7 4.2 fusion.131
  501.2 4.5 fusion.130
  507.3 6.6 multiply_reduce_fusion.8
  513.9 7.9 multiply_convert_fusion.5
  525.1 4.2 fusion.131
  536.5 4.5 fusion.130
  542.5 6.6 multiply_reduce_fusion.8
  549.2 7.9 multiply_convert_fusion.5
  560.3 4.2 fusion.131
  571.7 4.5 fusion.130
  577.8 6.6 multiply_reduce_fusion.8
  584.4 7.9 multiply_convert_fusion.5
  595.6 4.2 fusion.131
  606.7 3.9 fusion.61
  610.7 96.4 %reduce-scatter.9.cloned.1.call-done = bf16[8,1,256,128]{2,3,1,0:T(8,128)(2,1)} async-done(((bf16[8,1,4096,128]{2,3,1,0:T(8,128)(2,1)}), bf16[8,1,256,128]{2,3,1,0:T(8,128)(2,1)}) %reduce-scatter.9.cloned.1.call-update) | async-done | bytes 524304 | tf_op jit(solution)/shard_map/reduce_scatter | solution.py:210
  707.1 3.9 fusion.48
  711.0 104.7 %reduce-scatter.11.cloned.1.call-done = bf16[8,1,256,128]{2,3,1,0:T(8,128)(2,1)} async-done(((bf16[8,1,4096,128]{2,3,1,0:T(8,128)(2,1)}), bf16[8,1,256,128]{2,3,1,0:T(8,128)(2,1)}) %reduce-scatter.11.cloned.1.call-update) | async-done | bytes 524304 | tf_op jit(solution)/shard_map/reduce_scatter | solution.py:213
  815.8 3.9 fusion.46
  819.7 10.2 fusion.45
  831.0 10.9 fusion.40
  845.9 8.6 fusion.24
  858.1 39.7 %all-reduce.9 = (f32[1024]{0:T(1024)S(1)}, f32[1024]{0:T(1024)S(1)}, f32[1024]{0:T(1024)S(1)}, f32[4096]{0:T(1024)S(1)}, f32[1024]{0:T(1024)S(1)}, /*index=5*/f3...) all-reduce(f32[1024]{0:T(1024)S(1)} %bitcast.240, ...), channel_id=11, replica_groups=mesh['scene'=2,'seq'=16] {'scene','seq'}, use_global_device_ids=true, to_apply=%region_24.25.clone | all-reduce | flops 12288 | bytes 98304
  905.9 38.4 %reduce-scatter.13.cloned.1.call-done = f32[32,1024]{1,0:T(8,128)} async-done(((f32[1024,1024]{1,0:T(8,128)}), f32[32,1024]{1,0:T(8,128)}) %reduce-scatter.13.cloned.1.call-update) | async-done | bytes 131088 | tf_op jit(solution)/shard_map/reduce_scatter | solution.py:254
  944.2 140.0 %reduce-scatter.19.cloned.1.call-done = f32[32,1024]{1,0:T(8,128)} async-done(((f32[1024,1024]{1,0:T(8,128)}), f32[32,1024]{1,0:T(8,128)}) %reduce-scatter.19.cloned.1.call-update) | async-done | bytes 131088 | tf_op jit(solution)/shard_map/reduce_scatter | solution.py:257
  1084.2 140.4 %reduce-scatter.15.cloned.1.call-done = f32[32,1024]{1,0:T(8,128)} async-done(((f32[1024,1024]{1,0:T(8,128)}), f32[32,1024]{1,0:T(8,128)}) %reduce-scatter.15.cloned.1.call-update) | async-done | bytes 131088 | tf_op jit(solution)/shard_map/reduce_scatter | solution.py:255
  1224.7 140.2 %reduce-scatter.17.cloned.1.call-done = f32[32,1024]{1,0:T(8,128)} async-done(((f32[1024,1024]{1,0:T(8,128)}), f32[32,1024]{1,0:T(8,128)}) %reduce-scatter.17.cloned.1.call-update) | async-done | bytes 131088 | tf_op jit(solution)/shard_map/reduce_scatter | solution.py:256
  1364.8 199.7 %reduce-scatter.21.cloned.1.call-done = f32[32,4096]{1,0:T(8,128)} async-done(((f32[1024,4096]{1,0:T(8,128)}), f32[32,4096]{1,0:T(8,128)}) %reduce-scatter.21.cloned.1.call-update) | async-done | bytes 524304 | tf_op jit(solution)/shard_map/reduce_scatter | solution.py:263
  1564.5 187.9 %reduce-scatter.23.cloned.1.call-done = f32[128,1024]{1,0:T(8,128)} async-done(((f32[4096,1024]{1,0:T(8,128)}), f32[128,1024]{1,0:T(8,128)}) %reduce-scatter.23.cloned.1.call-update) | async-done | bytes 524304 | tf_op jit(solution)/shard_map/reduce_scatter | solution.py:264
  (414 shorter events, 261.2 us)
Async XLA Ops:
  7.2 128.0 %copy-start.2 = (bf16[1,256,1024]{2,1,0:T(8,128)(2,1)S(1)}, bf16[1,256,1024]{2,1,0:T(8,128)(2,1)}, u32[]{:S(2)}) copy-start(bf16[1,256,1024]{2,1,0:T(8,128)(2,1)} %param.22) | copy-start | bytes 1572868
  7.2 128.0 %copy-start.43 = (f32[1024]{0:T(1024)S(1)}, f32[1024]{0:T(1024)}, u32[]{:S(2)}) copy-start(f32[1024]{0:T(1024)} %param.37) | copy-start | bytes 12292
  7.2 128.0 %copy-start.38 = (f32[1024]{0:T(1024)S(1)}, f32[1024]{0:T(1024)}, u32[]{:S(2)}) copy-start(f32[1024]{0:T(1024)} %param.36) | copy-start | bytes 12292
  7.2 128.0 %copy-start.58 = (f32[1024]{0:T(1024)S(1)}, f32[1024]{0:T(1024)}, u32[]{:S(2)}) copy-start(f32[1024]{0:T(1024)} %param.31) | copy-start | bytes 12292
  7.2 201.2 %all-gather.3.cloned.1.call-start = ((), (), s32[]{:S(2)}) async-start(), calls=%async_computation.16 | async-start | bytes 8912896 | tf_op jit(solution)/shard_map/all_gather | solution.py:176
  8.6 131.8 %copy-start.56 = (s32[1,256]{1,0:T(1,128)S(1)}, s32[1,256]{1,0:T(1,128)}, u32[]{:S(2)}) copy-start(s32[1,256]{1,0:T(1,128)} %param.23) | copy-start | bytes 3076
  8.7 140.5 %copy-start.41 = (f32[256]{0:T(256)}, f32[256]{0:T(256)S(1)}, u32[]{:S(2)}) copy-start(f32[256]{0:T(256)S(1)} %broadcast_multiply_fusion.1) | copy-start | bytes 3076
  10.0 139.1 %copy-start.45 = (f32[256]{0:T(256)}, f32[256]{0:T(256)S(1)}, u32[]{:S(2)}) copy-start(f32[256]{0:T(256)S(1)} %fusion.42) | copy-start | bytes 3076
  12.7 694.4 %reduce-scatter.9.cloned.1.call-start = ((), (), s32[]{:S(2)}) async-start(), calls=%async_computation.8 | async-start | bytes 8912896 | tf_op jit(solution)/shard_map/reduce_scatter | solution.py:210
  15.3 8.0 collective-permute-start
  23.3 16.9 copy-start.16
  23.3 12.5 collective-permute-start.1
  25.8 14.3 collective-permute-start.8
  35.7 38.8 %copy-start.20 = (bf16[1,256,1024]{2,1,0:T(8,128)(2,1)}, bf16[1,256,1024]{2,1,0:T(8,128)(2,1)S(1)}, u32[]{:S(2)}) copy-start(bf16[1,256,1024]{2,1,0:T(8,128)(2,1)S(1)} %collective-permute-done.1) | copy-start | bytes 1572868
  35.7 12.3 collective-permute-start.2
  40.2 34.4 %collective-permute-start.9 = (bf16[1,256,1024]{2,1,0:T(8,128)(2,1)S(1)}, bf16[1,256,1024]{2,1,0:T(8,128)(2,1)S(1)}, u32[]{:S(2)}, u32[]{:S(2)}) collective-permute-start(bf16[1,256,1024]{2,1,0:T(8,128)(2,1)S(1)} %collective-permute-done.8), channel_id=1, source_target_pairs={{0,15},{1,0},{2,1},{3,2},{4,3},{5,4},{6,5},{7,6},{8,7},{9,8},{10,9... | collective-permute-start | bytes 1572872 | tf_op jit(solution)/shard_map/ppermute | solution.py:21
  48.1 57.0 %copy-start.24 = (bf16[1,256,1024]{2,1,0:T(8,128)(2,1)}, bf16[1,256,1024]{2,1,0:T(8,128)(2,1)S(1)}, u32[]{:S(2)}) copy-start(bf16[1,256,1024]{2,1,0:T(8,128)(2,1)S(1)} %collective-permute-done.2) | copy-start | bytes 1572868
  48.1 27.3 %collective-permute-start.3 = (bf16[1,256,1024]{2,1,0:T(8,128)(2,1)S(1)}, bf16[1,256,1024]{2,1,0:T(8,128)(2,1)S(1)}, u32[]{:S(2)}, u32[]{:S(2)}) collective-permute-start(bf16[1,256,1024]{2,1,0:T(8,128)(2,1)S(1)} %collective-permute-done.2), channel_id=1, source_target_pairs={{0,1},{1,2},{2,3},{3,4},{4,5},{5,6},{6,7},{7,8},{8,9},{9,10},{10,1... | collective-permute-start | bytes 1572872 | tf_op jit(solution)/shard_map/ppermute | solution.py:19
  74.6 30.5 %collective-permute-start.10 = (bf16[1,256,1024]{2,1,0:T(8,128)(2,1)S(1)}, bf16[1,256,1024]{2,1,0:T(8,128)(2,1)S(1)}, u32[]{:S(2)}, u32[]{:S(2)}) collective-permute-start(bf16[1,256,1024]{2,1,0:T(8,128)(2,1)S(1)} %collective-permute-done.9), channel_id=1, source_target_pairs={{0,15},{1,0},{2,1},{3,2},{4,3},{5,4},{6,5},{7,6},{8,7},{9,8},{10,9... | collective-permute-start | bytes 1572872 | tf_op jit(solution)/shard_map/ppermute | solution.py:21
  75.4 58.0 %copy-start.30 = (bf16[1,256,1024]{2,1,0:T(8,128)(2,1)}, bf16[1,256,1024]{2,1,0:T(8,128)(2,1)S(1)}, u32[]{:S(2)}) copy-start(bf16[1,256,1024]{2,1,0:T(8,128)(2,1)S(1)} %collective-permute-done.3) | copy-start | bytes 1572868
  75.4 30.5 %collective-permute-start.4 = (bf16[1,256,1024]{2,1,0:T(8,128)(2,1)S(1)}, bf16[1,256,1024]{2,1,0:T(8,128)(2,1)S(1)}, u32[]{:S(2)}, u32[]{:S(2)}) collective-permute-start(bf16[1,256,1024]{2,1,0:T(8,128)(2,1)S(1)} %collective-permute-done.3), channel_id=1, source_target_pairs={{0,1},{1,2},{2,3},{3,4},{4,5},{5,6},{6,7},{7,8},{8,9},{9,10},{10,1... | collective-permute-start | bytes 1572872 | tf_op jit(solution)/shard_map/ppermute | solution.py:19
  105.1 9.7 collective-permute-start.11
  105.9 27.5 %copy-start.32 = (bf16[1,256,1024]{2,1,0:T(8,128)(2,1)}, bf16[1,256,1024]{2,1,0:T(8,128)(2,1)S(1)}, u32[]{:S(2)}) copy-start(bf16[1,256,1024]{2,1,0:T(8,128)(2,1)S(1)} %collective-permute-done.4) | copy-start | bytes 1572868
  105.9 11.9 collective-permute-start.5
  115.6 17.7 %collective-permute-start.12 = (bf16[1,256,1024]{2,1,0:T(8,128)(2,1)S(1)}, bf16[1,256,1024]{2,1,0:T(8,128)(2,1)}, u32[]{:S(2)}, u32[]{:S(2)}) collective-permute-start(bf16[1,256,1024]{2,1,0:T(8,128)(2,1)S(1)} %collective-permute-done.11), channel_id=1, source_target_pairs={{0,15},{1,0},{2,1},{3,2},{4,3},{5,4},{6,5},{7,6},{8,7},{9,8},{10,9... | collective-permute-start | bytes 1572872 | tf_op jit(solution)/shard_map/ppermute | solution.py:21
  117.8 15.6 copy-start.34
  117.8 15.6 collective-permute-start.6
  133.4 8.9 collective-permute-start.13
  133.4 13.9 collective-permute-start.7
  140.4 23.1 %copy-start.19 = (bf16[1,256,1024]{2,1,0:T(8,128)(2,1)S(1)}, bf16[1,256,1024]{2,1,0:T(8,128)(2,1)}, u32[]{:S(2)}) copy-start(bf16[1,256,1024]{2,1,0:T(8,128)(2,1)} %copy-done.18) | copy-start | bytes 1572868
  140.4 24.0 %copy-start.23 = (bf16[1,256,1024]{2,1,0:T(8,128)(2,1)S(1)}, bf16[1,256,1024]{2,1,0:T(8,128)(2,1)}, u32[]{:S(2)}) copy-start(bf16[1,256,1024]{2,1,0:T(8,128)(2,1)} %copy-done.22) | copy-start | bytes 1572868
  140.4 24.8 %copy-start.27 = (bf16[1,256,1024]{2,1,0:T(8,128)(2,1)S(1)}, bf16[1,256,1024]{2,1,0:T(8,128)(2,1)}, u32[]{:S(2)}) copy-start(bf16[1,256,1024]{2,1,0:T(8,128)(2,1)} %copy-done.26) | copy-start | bytes 1572868
  140.4 25.6 %copy-start.29 = (bf16[1,256,1024]{2,1,0:T(8,128)(2,1)S(1)}, bf16[1,256,1024]{2,1,0:T(8,128)(2,1)}, u32[]{:S(2)}) copy-start(bf16[1,256,1024]{2,1,0:T(8,128)(2,1)} %copy-done.28) | copy-start | bytes 1572868
  142.3 28.4 %collective-permute-start.14 = (bf16[1,256,1024]{2,1,0:T(8,128)(2,1)}, bf16[1,256,1024]{2,1,0:T(8,128)(2,1)S(1)}, u32[]{:S(2)}, u32[]{:S(2)}) collective-permute-start(bf16[1,256,1024]{2,1,0:T(8,128)(2,1)} %collective-permute-done.13), channel_id=1, source_target_pairs={{0,15},{1,0},{2,1},{3,2},{4,3},{5,4},{6,5},{7,6},{8,7},{9,8},{10,9... | collective-permute-start | bytes 1572872 | tf_op jit(solution)/shard_map/ppermute | solution.py:21
  151.0 24.3 %copy-start.35 = (bf16[1,256,1024]{2,1,0:T(8,128)(2,1)S(1)}, bf16[1,256,1024]{2,1,0:T(8,128)(2,1)}, u32[]{:S(2)}) copy-start(bf16[1,256,1024]{2,1,0:T(8,128)(2,1)} %copy-done.34) | copy-start | bytes 1572868
  153.0 23.1 %copy-start.33 = (bf16[1,256,1024]{2,1,0:T(8,128)(2,1)S(1)}, bf16[1,256,1024]{2,1,0:T(8,128)(2,1)}, u32[]{:S(2)}) copy-start(bf16[1,256,1024]{2,1,0:T(8,128)(2,1)} %copy-done.32) | copy-start | bytes 1572868
  154.9 22.1 %copy-start.31 = (bf16[1,256,1024]{2,1,0:T(8,128)(2,1)S(1)}, bf16[1,256,1024]{2,1,0:T(8,128)(2,1)}, u32[]{:S(2)}) copy-start(bf16[1,256,1024]{2,1,0:T(8,128)(2,1)} %copy-done.30) | copy-start | bytes 1572868
  156.8 20.9 %copy-start.25 = (bf16[1,256,1024]{2,1,0:T(8,128)(2,1)S(1)}, bf16[1,256,1024]{2,1,0:T(8,128)(2,1)}, u32[]{:S(2)}) copy-start(bf16[1,256,1024]{2,1,0:T(8,128)(2,1)} %copy-done.24) | copy-start | bytes 1572868
  158.8 19.8 %copy-start.21 = (bf16[1,256,1024]{2,1,0:T(8,128)(2,1)S(1)}, bf16[1,256,1024]{2,1,0:T(8,128)(2,1)}, u32[]{:S(2)}) copy-start(bf16[1,256,1024]{2,1,0:T(8,128)(2,1)} %copy-done.20) | copy-start | bytes 1572868
  160.7 18.7 %copy-start.17 = (bf16[1,256,1024]{2,1,0:T(8,128)(2,1)S(1)}, bf16[1,256,1024]{2,1,0:T(8,128)(2,1)}, u32[]{:S(2)}) copy-start(bf16[1,256,1024]{2,1,0:T(8,128)(2,1)} %copy-done.16) | copy-start | bytes 1572868
  220.2 71.4 %copy-start.47 = (f32[1024]{0:T(1024)S(1)}, f32[1024]{0:T(1024)}, u32[]{:S(2)}) copy-start(f32[1024]{0:T(1024)} %param.33) | copy-start | bytes 12292
  220.2 74.3 %copy-start.37 = (f32[1024]{0:T(1024)S(1)}, f32[1024]{0:T(1024)}, u32[]{:S(2)}) copy-start(f32[1024]{0:T(1024)} %param.38) | copy-start | bytes 12292
  220.2 74.3 %copy-start.40 = (f32[1024]{0:T(1024)S(1)}, f32[1024]{0:T(1024)}, u32[]{:S(2)}) copy-start(f32[1024]{0:T(1024)} %param.39) | copy-start | bytes 12292
  220.2 74.3 %copy-start.57 = (f32[4096]{0:T(1024)S(1)}, f32[4096]{0:T(1024)}, u32[]{:S(2)}) copy-start(f32[4096]{0:T(1024)} %param.34) | copy-start | bytes 49156
  291.5 9.0 copy-start.10
  291.6 9.0 slice-start.2
  294.2 12.9 copy-start.4
  294.6 12.6 slice-start
  322.4 15.0 copy-start.1
  357.6 15.0 copy-start.1
  393.0 15.0 copy-start.1
  428.3 15.0 copy-start.1
  463.5 15.0 copy-start.1
  498.9 15.0 copy-start.1
  534.1 15.0 copy-start.1
  569.4 15.0 copy-start.1
  602.3 213.5 %reduce-scatter.11.cloned.1.call-start = ((), (), s32[]{:S(2)}) async-start(), calls=%async_computation.9 | async-start | bytes 8912896 | tf_op jit(solution)/shard_map/reduce_scatter | solution.py:213
  603.0 341.2 %reduce-scatter.13.cloned.1.call-start = ((), (), s32[]{:S(2)}) async-start(), calls=%async_computation.10 | async-start | bytes 4325376 | tf_op jit(solution)/shard_map/reduce_scatter | solution.py:254
  606.4 477.8 %reduce-scatter.19.cloned.1.call-start = ((), (), s32[]{:S(2)}) async-start(), calls=%async_computation.13 | async-start | bytes 4325376 | tf_op jit(solution)/shard_map/reduce_scatter | solution.py:257
  610.6 614.0 %reduce-scatter.15.cloned.1.call-start = ((), (), s32[]{:S(2)}) async-start(), calls=%async_computation.11 | async-start | bytes 4325376 | tf_op jit(solution)/shard_map/reduce_scatter | solution.py:255
  711.0 653.8 %reduce-scatter.17.cloned.1.call-start = ((), (), s32[]{:S(2)}) async-start(), calls=%async_computation.12 | async-start | bytes 4325376 | tf_op jit(solution)/shard_map/reduce_scatter | solution.py:256
  819.7 744.8 %reduce-scatter.21.cloned.1.call-start = ((), (), s32[]{:S(2)}) async-start(), calls=%async_computation.14 | async-start | bytes 17301504 | tf_op jit(solution)/shard_map/reduce_scatter | solution.py:263
  830.0 922.4 %reduce-scatter.23.cloned.1.call-start = ((), (), s32[]{:S(2)}) async-start(), calls=%async_computation.15 | async-start | bytes 17301504 | tf_op jit(solution)/shard_map/reduce_scatter | solution.py:264
  854.5 48.5 %copy-start.51 = (f32[256]{0:T(256)S(1)}, f32[256]{0:T(256)}, u32[]{:S(2)}) copy-start(f32[256]{0:T(256)} %copy-done.50) | copy-start | bytes 3076
  (31 other events, 102.8 us)
Sparse Core Ops, SparseCore 0:
  12.8 115.3 all-gather.2
  602.4 104.6 reduce-scatter.8
  711.1 104.5 reduce-scatter.10
  818.5 125.7 reduce-scatter.12
  946.9 137.2 reduce-scatter.18
  1086.9 137.6 reduce-scatter.14
  1227.5 137.2 reduce-scatter.16
  1367.7 196.7 reduce-scatter.20
  1567.4 184.9 reduce-scatter.22
